TPU v7x, 128 devices: a whole 4x4x4 slice. The times are simulated.
128 devices in a mesh: gx: 8 (over y, core), gy: 4 (over z), gz: 4 (over x).
Axes of the slice: x: 4, y: 4, z: 4, core: 2. Of those that a mesh axis runs over, the one named last changes fastest.
Arguments:
- right_side: float32 [128, 64, 1024], P('gx', 'gy', 'gz'), may hold values from -8 to 8
- conductance: float32 [3, 128, 64, 1024], P(None, 'gx', 'gy', 'gz'), may hold values from 0.2 to 5
- storage: float32 [128, 64, 1024], P('gx', 'gy', 'gz'), may hold values from 0.05 to 0.8
- dirichlet: int32 [128, 64, 1024], P('gx', 'gy', 'gz'), may hold values 0 or 1
- basis: float32 [16, 128, 64, 1024], P(None, 'gx', 'gy', 'gz'), may hold values from -2 to 2
- coarse_inverse: float32 [2048, 2048], P(('gx', 'gy', 'gz')), may hold values from 0 to 2, as said below
Outputs:
- solution_field: float32 [128, 64, 1024], P('gx', 'gy', 'gz')
- residual: float32 [128, 64, 1024], P('gx', 'gy', 'gz')
Inputs may be any that keep to these rules, and one draw needn't show every extreme that they name: `coarse_inverse`: symmetric positive definite.
All inputs are finite; a program needn't handle non-finite values. No bound on the sum of `dirichlet` on one device may be relied on, other than what follows from the above.
Results may differ from a plain program's by a relative error of at most 0.0003.
Values sent between devices are 32-bit elements; how exact they have to be, the bound alone decides.
A program may use at most 128 MiB of HBM per device.

v0:
```python
import jax
import jax.numpy as jnp
from jax import lax
from jax.sharding import PartitionSpec as P

SWEEPS = 4
ITERS = 2
RELAX = 2.0 / 3.0


def padded(value, sides, width):
    for axis, dim in sides:
        count, length = (lax.axis_size(axis), value.shape[dim])
        up = [(i, (i + 1) % count) for i in range(count - 1)]
        down = [(j, i) for i, j in up]
        last = lax.slice_in_dim(value, length - width, length, axis=dim)
        leading = lax.slice_in_dim(value, 0, width, axis=dim)
        before = lax.ppermute(last, axis, up)
        after = lax.ppermute(leading, axis, down)
        value = jnp.concatenate([before, value, after], axis=dim)
    return value


def pad_cond(cond):
    return jnp.pad(cond, ((0, 0), (1, 1), (1, 1), (1, 1)))


def stencil(padded_free, padded_cond, field, storage, free):
    middle = padded_free[1:-1, 1:-1, 1:-1]
    total = storage * middle
    total = (
        total
        + padded_cond[0, 1:-1, 1:-1, 1:-1] * (middle - padded_free[2:, 1:-1, 1:-1])
        + padded_cond[0, :-2, 1:-1, 1:-1] * (middle - padded_free[:-2, 1:-1, 1:-1])
    )
    total = (
        total
        + padded_cond[1, 1:-1, 1:-1, 1:-1] * (middle - padded_free[1:-1, 2:, 1:-1])
        + padded_cond[1, 1:-1, :-2, 1:-1] * (middle - padded_free[1:-1, :-2, 1:-1])
    )
    total = (
        total
        + padded_cond[2, 1:-1, 1:-1, 1:-1] * (middle - padded_free[1:-1, 1:-1, 2:])
        + padded_cond[2, 1:-1, 1:-1, :-2] * (middle - padded_free[1:-1, 1:-1, :-2])
    )
    return free * total + (1.0 - free) * field


def diagonal_of(padded_cond, storage, free):
    total = storage + padded_cond[0, 1:-1, 1:-1, 1:-1] + padded_cond[0, :-2, 1:-1, 1:-1]
    total = total + padded_cond[1, 1:-1, 1:-1, 1:-1] + padded_cond[1, 1:-1, :-2, 1:-1]
    total = total + padded_cond[2, 1:-1, 1:-1, 1:-1] + padded_cond[2, 1:-1, 1:-1, :-2]
    return free * total + (1.0 - free)


def jacobi(rhs_box, padded_cond, diagonal, storage_box, free_box):
    guess = jnp.zeros_like(rhs_box)
    for sweep in range(SWEEPS):
        image = stencil(jnp.pad(free_box * guess, 1), padded_cond, guess, storage_box, free_box)
        guess = guess + RELAX * (rhs_box - image) / diagonal
    return guess


def project(basis, field):
    return jnp.dot(
        basis.reshape(basis.shape[0], -1), field.reshape(-1), precision=lax.Precision.HIGHEST
    )


def expand(basis, weights, field):
    return jnp.dot(
        weights, basis.reshape(basis.shape[0], -1), precision=lax.Precision.HIGHEST
    ).reshape(field.shape)


def gather_coarse(values):
    return lax.all_gather(values, ("gx", "gy", "gz"), axis=0, tiled=True)


def residual_rim(field):
    return padded(field, (("gx", 0), ("gy", 1), ("gz", 2)), 2)


def norm_sum(value):
    return lax.psum(value, ("gx", "gy", "gz"))


def shards(right_side, conductance, storage, dirichlet, basis, coarse_inverse):
    free = 1.0 - dirichlet.astype(jnp.float32)
    stacked = jnp.concatenate([conductance, storage[None], free[None]], axis=0)
    wide = padded(stacked, (("gx", 1), ("gy", 2), ("gz", 3)), 3)
    cond_face = wide[:3, 2:-2, 2:-2, 2:-2]
    free_face = wide[4, 2:-2, 2:-2, 2:-2]
    cond_box = wide[:3, 1:-1, 1:-1, 1:-1]
    storage_box = wide[3, 1:-1, 1:-1, 1:-1]
    free_box = wide[4, 1:-1, 1:-1, 1:-1]
    box_cond = pad_cond(cond_box)
    box_diag = diagonal_of(box_cond, storage_box, free_box)

    def schwarz(rhs_box):
        return jacobi(rhs_box, box_cond, box_diag, storage_box, free_box)[2:-2, 2:-2, 2:-2]

    solution = jnp.zeros_like(right_side)
    residual = right_side
    rhs_box = residual_rim(residual)
    coarse_now = project(basis, residual)
    weights = jnp.dot(coarse_inverse, gather_coarse(coarse_now), precision=lax.Precision.HIGHEST)
    precond = schwarz(rhs_box) + expand(basis, weights, residual)
    norm_now = norm_sum(jnp.sum(residual * precond))
    direction = precond
    for step in range(ITERS):
        near_dir = padded(direction, (("gx", 0), ("gy", 1), ("gz", 2)), 1)
        image = stencil(free_face * near_dir, cond_face, direction, storage, free)
        local_curve = jnp.sum(direction * image)
        curvature = lax.psum(local_curve, ("gx", "gy", "gz"))
        alpha = norm_now / curvature
        solution = solution + alpha * direction
        residual = residual - alpha * image
        if step + 1 < ITERS:
            rhs_box = residual_rim(residual)
            coarse_now = project(basis, residual)
            gathered = gather_coarse(coarse_now)
            weights = jnp.dot(coarse_inverse, gathered, precision=lax.Precision.HIGHEST)
            precond = schwarz(rhs_box) + expand(basis, weights, residual)
            norm_next = norm_sum(jnp.sum(residual * precond))
            direction = precond + norm_next / norm_now * direction
            norm_now = norm_next
    return (solution, residual)


def solution(mesh):
    placed = (
        P("gx", "gy", "gz"),
        P(None, "gx", "gy", "gz"),
        P("gx", "gy", "gz"),
        P("gx", "gy", "gz"),
        P(None, "gx", "gy", "gz"),
        P(("gx", "gy", "gz"), None),
    )
    return jax.shard_map(
        shards,
        mesh=mesh,
        in_specs=placed,
        out_specs=(P("gx", "gy", "gz"), P("gx", "gy", "gz")),
        check_vma=False,
    )
```

profile of v0, /device:TPU:1, one launch (start us, length us, event | category | flops | bytes accessed | tf_op | source)
XLA Modules:
  0.0 572.3 jit_solution(1241836847515531308)
XLA Ops:
  2.9 4.6 collective-permute-start.6
  10.3 3.6 collective-permute-start
  15.8 8.8 %fusion.8 = f32[16]{0:T(128)S(1)} fusion(f32[16,16,16,256]{3,2,1,0:T(8,128)} %param.10, f32[16,16,256,1]{2,1,0,3:T(8,128)} %bitcast.289), kind=kOutput, calls=%fused_computation.14 | convolution fusion | flops 12582912 | bytes 4456512 | tf_op jit(solution)/shard_map/dot_general | solution.py:65
  24.8 66.8 %all-reduce.8 = f32[2048]{0:T(1024)S(1)} all-reduce(f32[2048]{0:T(1024)S(1)} %dynamic-update-slice), channel_id=1, replica_groups=mesh['gx'=8,'gy'=4,'gz'=4] {'gx','gy','gz'}, use_global_device_ids=true, to_apply=%add.8 | all-reduce | flops 2048 | bytes 16384
  92.0 2.4 collective-permute-start.2
  98.7 4.7 collective-permute-start.8
  105.7 5.1 fusion.2
  110.9 8.1 %copy.37 = f32[5,22,16,256]{2,1,3,0:T(8,128)} copy(f32[5,22,16,256]{3,2,1,0:T(8,128)S(1)} %pad_maximum_fusion.2) | data formatting | bytes 3604480 | tf_op jit(solution)/shard_map/concatenate | solution.py:20
  119.0 9.0 %copy.36 = f32[5,22,3,256]{2,1,3,0:T(8,128)} copy(f32[5,22,3,256]{3,1,2,0:T(8,128)} %collective-permute-done.8) | data formatting | bytes 675840 | tf_op jit(solution)/shard_map/ppermute | solution.py:18
  128.0 9.0 %copy.38 = f32[5,22,3,256]{2,1,3,0:T(8,128)} copy(f32[5,22,3,256]{3,1,2,0:T(8,128)} %collective-permute-done.9) | data formatting | bytes 675840 | tf_op jit(solution)/shard_map/ppermute | solution.py:19
  137.0 16.9 %pad_maximum_fusion = f32[5,22,22,256]{2,1,3,0:T(8,128)S(1)} fusion(f32[5,22,3,256]{2,1,3,0:T(8,128)} %copy.38, f32[5,22,16,256]{2,1,3,0:T(8,128)} %copy.37, f32[5,22,3,256]{2,1,3,0:T(8,128)} %copy.36), kind=kLoop, calls=%fused_computation | loop fusion | flops 1239040 | bytes 4956160 | tf_op jit(solution)/shard_map/concatenate | solution.py:20
  153.8 5.4 copy-done.4
  160.0 2.7 collective-permute-start.10
  164.9 4.0 collective-permute-start.4
  170.4 9.2 %copy.40 = f32[5,22,22,256]{3,2,1,0:T(8,128)S(1)} copy(f32[5,22,22,256]{2,1,3,0:T(8,128)} %copy-done.4) | data formatting | bytes 4956160 | tf_op jit(solution)/shard_map/concatenate | solution.py:20
  179.6 3.1 copy.39
  184.6 3.2 pad_maximum_fusion.1
  191.2 3.7 fusion.213
  196.9 2.7 fusion.217
  201.5 2.1 fusion.208
  203.7 4.9 collective-permute-start.12
  208.6 2.3 collective-permute-start.13
  210.9 2.7 collective-permute-done.13
  213.7 4.3 collective-permute-start.14
  219.3 3.2 collective-permute-done.15
  222.7 4.3 collective-permute-start.16
  229.4 2.7 collective-permute-done.16
  232.2 3.9 collective-permute-done.17
  236.8 2.2 multiply_reduce_fusion.2
  239.0 63.0 %all-reduce.10 = (f32[]{:T(128)}, f32[]{:T(128)}) all-reduce(f32[]{:T(128)} %get-tuple-element.5, f32[]{:T(128)} %get-tuple-element.4), channel_id=1, replica_groups=mesh['gx'=8,'gy'=4,'gz'=4] {'gx','gy','gz'}, use_global_device_ids=true, to_apply=%region_1.2 | all-reduce | flops 2 | bytes 16 | tf_op jit(solution)/shard_map/psum | solution.py:85
  304.5 3.0 collective-permute-start.18
  309.4 8.6 %fusion.11 = f32[16]{0:T(128)S(1)} fusion(f32[16,16,16,256]{3,2,1,0:T(8,128)} %param.10, f32[16,16,256,1]{2,1,0,3:T(8,128)S(1)} %bitcast.285), kind=kOutput, calls=%fused_computation.15 | convolution fusion | flops 12582912 | bytes 4456512 | tf_op jit(solution)/shard_map/dot_general | solution.py:65
  318.3 63.0 %all-reduce.9 = f32[2048]{0:T(1024)S(1)} all-reduce(f32[2048]{0:T(1024)S(1)} %dynamic-update-slice.1), channel_id=1, replica_groups=mesh['gx'=8,'gy'=4,'gz'=4] {'gx','gy','gz'}, use_global_device_ids=true, to_apply=%add.9 | all-reduce | flops 2048 | bytes 16384
  381.4 2.7 collective-permute-start.20
  385.6 3.2 collective-permute-done.21
  392.3 6.4 %fusion = f32[1,16,16,256]{3,0,2,1:T(1,128)S(1)} fusion(f32[16,1,1,1]{0,1,3,2:T(1,128)S(1)} %convolution_bitcast_fusion, f32[16,16,256,16]{2,1,0,3:T(8,128)} %bitcast.283), kind=kOutput, calls=%fused_computation.2 | convolution fusion | flops 12582912 | bytes 4456512 | tf_op jit(solution)/shard_map/dot_general | solution.py:71
  399.5 2.0 fusion.216
  405.1 2.5 multiply_reduce_fusion.1
  407.6 67.1 %psum.30 = f32[]{:T(128)} all-reduce(f32[]{:T(128)} %get-tuple-element.10), channel_id=1, replica_groups=mesh['gx'=8,'gy'=4,'gz'=4] {'gx','gy','gz'}, use_global_device_ids=true, to_apply=%region_5.6 | all-reduce | flops 1 | bytes 8 | tf_op jit(solution)/shard_map/psum | solution.py:85
  476.9 2.3 collective-permute-start.24
  479.1 2.1 collective-permute-start.25
  481.2 3.0 collective-permute-done.25
  484.2 2.3 collective-permute-start.26
  488.0 3.2 collective-permute-done.27
  494.6 3.9 collective-permute-done.28
  498.5 3.9 collective-permute-done.29
  504.2 2.4 multiply_reduce_fusion
  506.7 63.2 %psum.31 = f32[]{:T(128)} all-reduce(f32[]{:T(128)} %get-tuple-element.8), channel_id=1, replica_groups=mesh['gx'=8,'gy'=4,'gz'=4] {'gx','gy','gz'}, use_global_device_ids=true, to_apply=%region_7.8 | all-reduce | flops 1 | bytes 8 | tf_op jit(solution)/shard_map/psum | solution.py:115
  (146 shorter events, 53.1 us)
Async XLA Ops:
  0.6 91.0 %copy-start = (f32[16,2048]{1,0:T(8,128)S(1)}, f32[16,2048]{1,0:T(8,128)}, u32[]{:S(2)}) copy-start(f32[16,2048]{1,0:T(8,128)} %param.11) | copy-start | bytes 393220
  0.6 95.8 %copy-start.15 = (f32[16,16,256]{2,1,0:T(8,128)S(1)}, f32[16,16,256]{2,1,0:T(8,128)}, u32[]{:S(2)}) copy-start(f32[16,16,256]{2,1,0:T(8,128)} %param.8) | copy-start | bytes 786436
  0.7 95.8 %copy-start.7 = (f32[3,16,16,256]{3,2,1,0:T(8,128)S(1)}, f32[3,16,16,256]{3,2,1,0:T(8,128)}, u32[]{:S(2)}) copy-start(f32[3,16,16,256]{3,2,1,0:T(8,128)} %param.7) | copy-start | bytes 2359300
  0.7 91.3 %copy-start.16 = (f32[16,16,256]{2,1,0:T(8,128)S(1)}, f32[16,16,256]{2,1,0:T(8,128)}, u32[]{:S(2)}) copy-start(f32[16,16,256]{2,1,0:T(8,128)} %param.6) | copy-start | bytes 786436
  1.8 95.9 %copy-start.18 = (f32[1,16,16,256]{3,2,1,0:T(8,128)}, f32[1,16,16,256]{3,2,1,0:T(8,128)S(1)}, u32[]{:S(2)}) copy-start(f32[1,16,16,256]{3,2,1,0:T(8,128)S(1)} %fusion.212) | copy-start | bytes 786436
  2.9 92.8 %collective-permute-start.6 = (f32[5,3,16,256]{3,2,1,0:T(8,128)S(1)}, f32[5,3,16,256]{3,2,1,0:T(8,128)S(1)}, u32[]{:S(2)}, u32[]{:S(2)}) collective-permute-start(f32[5,3,16,256]{3,2,1,0:T(8,128)S(1)} %get-tuple-element.36), channel_id=1, source_target_pairs={{0,16},{16,32},{32,48},{48,64},{64,80},{80,96},{96,112},{1,17},{17... | collective-permute-start | bytes 737288 | tf_op jit(solution)/shard_map/ppermute | solution.py:18
  7.6 88.9 %collective-permute-start.7 = (f32[5,3,16,256]{3,2,1,0:T(8,128)S(1)}, f32[5,3,16,256]{3,2,1,0:T(8,128)}, u32[]{:S(2)}, u32[]{:S(2)}) collective-permute-start(f32[5,3,16,256]{3,2,1,0:T(8,128)S(1)} %get-tuple-element.37), channel_id=1, source_target_pairs={{16,0},{32,16},{48,32},{64,48},{80,64},{96,80},{112,96},{17,1},{33... | collective-permute-start | bytes 737288 | tf_op jit(solution)/shard_map/ppermute | solution.py:19
  10.3 81.6 %collective-permute-start = (f32[2,16,256]{2,1,0:T(8,128)S(1)}, f32[2,16,256]{2,1,0:T(8,128)S(1)}, u32[]{:S(2)}, u32[]{:S(2)}) collective-permute-start(f32[2,16,256]{2,1,0:T(8,128)S(1)} %get-tuple-element.61), channel_id=1, source_target_pairs={{0,16},{16,32},{32,48},{48,64},{64,80},{80,96},{96,112},{1,17},{17... | collective-permute-start | bytes 98312 | tf_op jit(solution)/shard_map/ppermute | solution.py:18
  13.9 78.1 %collective-permute-start.1 = (f32[2,16,256]{2,1,0:T(8,128)S(1)}, f32[2,16,256]{2,1,0:T(8,128)S(1)}, u32[]{:S(2)}, u32[]{:S(2)}) collective-permute-start(f32[2,16,256]{2,1,0:T(8,128)S(1)} %get-tuple-element.60), channel_id=1, source_target_pairs={{16,0},{32,16},{48,32},{64,48},{80,64},{96,80},{112,96},{17,1},{33... | collective-permute-start | bytes 98312 | tf_op jit(solution)/shard_map/ppermute | solution.py:19
  92.0 18.8 %copy-start.22 = (f32[20,16,256]{2,1,0:T(8,128)}, f32[20,16,256]{2,1,0:T(8,128)S(1)}, u32[]{:S(2)}) copy-start(f32[20,16,256]{2,1,0:T(8,128)S(1)} %constant_dynamic-update-slice_fusion) | copy-start | bytes 983044
  92.0 18.7 %collective-permute-start.2 = (f32[20,2,256]{2,1,0:T(2,128)S(1)}, f32[20,2,256]{2,1,0:T(2,128)S(1)}, u32[]{:S(2)}, u32[]{:S(2)}) collective-permute-start(f32[20,2,256]{2,1,0:T(2,128)S(1)} %get-tuple-element.48), channel_id=1, source_target_pairs={{0,4},{4,8},{8,12},{1,5},{5,9},{9,13},{2,6},{6,10},{10,14},{3,7},{... | collective-permute-start | bytes 122888 | tf_op jit(solution)/shard_map/ppermute | solution.py:18
  94.5 16.3 %collective-permute-start.3 = (f32[20,2,256]{2,1,0:T(2,128)S(1)}, f32[20,2,256]{2,1,0:T(2,128)S(1)}, u32[]{:S(2)}, u32[]{:S(2)}) collective-permute-start(f32[20,2,256]{2,1,0:T(2,128)S(1)} %get-tuple-element.49), channel_id=1, source_target_pairs={{4,0},{8,4},{12,8},{5,1},{9,5},{13,9},{6,2},{10,6},{14,10},{7,3},{... | collective-permute-start | bytes 122888 | tf_op jit(solution)/shard_map/ppermute | solution.py:19
  98.7 20.3 %collective-permute-start.8 = (f32[5,22,3,256]{3,1,2,0:T(8,128)}, f32[5,22,3,256]{3,1,2,0:T(8,128)}, u32[]{:S(2)}, u32[]{:S(2)}) collective-permute-start(f32[5,22,3,256]{3,1,2,0:T(8,128)} %copy.55), channel_id=1, source_target_pairs={{0,4},{4,8},{8,12},{1,5},{5,9},{9,13},{2,6},{6,10},{10,14},{3,7},{... | collective-permute-start | bytes 1013768 | tf_op jit(solution)/shard_map/ppermute | solution.py:18
  104.3 23.8 %collective-permute-start.9 = (f32[5,22,3,256]{3,1,2,0:T(8,128)}, f32[5,22,3,256]{3,1,2,0:T(8,128)}, u32[]{:S(2)}, u32[]{:S(2)}) collective-permute-start(f32[5,22,3,256]{3,1,2,0:T(8,128)} %copy.56), channel_id=1, source_target_pairs={{4,0},{8,4},{12,8},{5,1},{9,5},{13,9},{6,2},{10,6},{14,10},{7,3},{... | collective-permute-start | bytes 1013768 | tf_op jit(solution)/shard_map/ppermute | solution.py:19
  160.0 19.6 %collective-permute-start.10 = (f32[5,22,22,3]{2,1,3,0:T(8,128)}, f32[5,22,22,3]{2,1,3,0:T(8,128)}, u32[]{:S(2)}, u32[]{:S(2)}) collective-permute-start(f32[5,22,22,3]{2,1,3,0:T(8,128)} %get-tuple-element.30), channel_id=1, source_target_pairs={{0,1},{1,2},{2,3},{4,5},{5,6},{6,7},{8,9},{9,10},{10,11},{12,13},{... | collective-permute-start | bytes 87128 | tf_op jit(solution)/shard_map/ppermute | solution.py:18
  162.7 20.0 %collective-permute-start.11 = (f32[5,22,22,3]{2,1,3,0:T(8,128)}, f32[5,22,22,3]{2,1,3,0:T(8,128)S(1)}, u32[]{:S(2)}, u32[]{:S(2)}) collective-permute-start(f32[5,22,22,3]{2,1,3,0:T(8,128)} %get-tuple-element.31), channel_id=1, source_target_pairs={{1,0},{2,1},{3,2},{5,4},{6,5},{7,6},{9,8},{10,9},{11,10},{13,12},{... | collective-permute-start | bytes 87128 | tf_op jit(solution)/shard_map/ppermute | solution.py:19
  164.9 25.7 %collective-permute-start.4 = (f32[20,20,2]{2,1,0:T(8,128)}, f32[20,20,2]{2,1,0:T(8,128)S(1)}, u32[]{:S(2)}, u32[]{:S(2)}) collective-permute-start(f32[20,20,2]{2,1,0:T(8,128)} %get-tuple-element.40), channel_id=1, source_target_pairs={{0,1},{1,2},{2,3},{4,5},{5,6},{6,7},{8,9},{9,10},{10,11},{12,13},{... | collective-permute-start | bytes 9608 | tf_op jit(solution)/shard_map/ppermute | solution.py:18
  168.9 22.4 %collective-permute-start.5 = (f32[20,20,2]{2,1,0:T(8,128)}, f32[20,20,2]{2,1,0:T(8,128)}, u32[]{:S(2)}, u32[]{:S(2)}) collective-permute-start(f32[20,20,2]{2,1,0:T(8,128)} %get-tuple-element.41), channel_id=1, source_target_pairs={{1,0},{2,1},{3,2},{5,4},{6,5},{7,6},{9,8},{10,9},{11,10},{13,12},{... | collective-permute-start | bytes 9608 | tf_op jit(solution)/shard_map/ppermute | solution.py:19
  187.8 48.3 %copy-start.1 = (f32[5,22,22,262]{3,2,1,0:T(8,128)}, f32[5,22,22,262]{3,2,1,0:T(8,128)S(1)}, u32[]{:S(2)}) copy-start(f32[5,22,22,262]{3,2,1,0:T(8,128)S(1)} %pad_maximum_fusion.1) | copy-start | bytes 7608484
  201.4 37.6 %copy-start.21 = (f32[20,20,260]{2,1,0:T(8,128)}, f32[20,20,260]{2,1,0:T(8,128)S(1)}, u32[]{:S(2)}) copy-start(f32[20,20,260]{2,1,0:T(8,128)S(1)} %get-tuple-element.32) | copy-start | bytes 1248004
  201.4 35.3 %copy-start.6 = (f32[5,22,22,256]{3,2,1,0:T(8,128)S(1)}, f32[5,22,22,256]{3,2,1,0:T(8,128)}, u32[]{:S(2)}) copy-start(f32[5,22,22,256]{3,2,1,0:T(8,128)} %copy-done.5) | copy-start | bytes 7434244
  201.4 35.3 %copy-start.8 = (f32[3,16,16,256]{3,2,1,0:T(8,128)S(1)}, f32[3,16,16,256]{3,2,1,0:T(8,128)}, u32[]{:S(2)}) copy-start(f32[3,16,16,256]{3,2,1,0:T(8,128)} %param.7) | copy-start | bytes 2359300
  201.4 35.3 %copy-start.12 = (f32[5,22,22,3]{3,2,1,0:T(8,128)S(1)}, f32[5,22,22,3]{3,2,1,0:T(8,128)}, u32[]{:S(2)}) copy-start(f32[5,22,22,3]{3,2,1,0:T(8,128)} %copy.39) | copy-start | bytes 87124
  201.5 35.3 %copy-start.17 = (f32[16,16,256]{2,1,0:T(8,128)S(1)}, f32[16,16,256]{2,1,0:T(8,128)}, u32[]{:S(2)}) copy-start(f32[16,16,256]{2,1,0:T(8,128)} %param.6) | copy-start | bytes 786436
  201.5 35.3 %copy-start.19 = (f32[1,16,16,256]{3,2,1,0:T(8,128)S(1)}, f32[1,16,16,256]{3,2,1,0:T(8,128)}, u32[]{:S(2)}) copy-start(f32[1,16,16,256]{3,2,1,0:T(8,128)} %copy-done.18) | copy-start | bytes 786436
  201.5 35.3 %copy-start.20 = (s32[16,16,256]{2,1,0:T(8,128)S(1)}, s32[16,16,256]{2,1,0:T(8,128)}, u32[]{:S(2)}) copy-start(s32[16,16,256]{2,1,0:T(8,128)} %param.9) | copy-start | bytes 786436
  201.5 35.3 %copy-start.26 = (f32[5,3,16,256]{3,2,1,0:T(8,128)S(1)}, f32[5,3,16,256]{3,2,1,0:T(8,128)}, u32[]{:S(2)}) copy-start(f32[5,3,16,256]{3,2,1,0:T(8,128)} %copy-done.25) | copy-start | bytes 737284
  203.7 35.4 %copy-start.10 = (f32[16,16,256]{2,1,0:T(8,128)}, f32[16,16,256]{2,1,0:T(8,128)S(1)}, u32[]{:S(2)}) copy-start(f32[16,16,256]{2,1,0:T(8,128)S(1)} %fusion.208) | copy-start | bytes 786436
  203.7 7.3 %collective-permute-start.12 = (f32[1,16,256]{2,1,0:T(8,128)S(1)}, f32[1,16,256]{2,1,0:T(8,128)S(1)}, u32[]{:S(2)}, u32[]{:S(2)}) collective-permute-start(f32[1,16,256]{2,1,0:T(8,128)S(1)} %get-tuple-element.58), channel_id=1, source_target_pairs={{0,16},{16,32},{32,48},{48,64},{64,80},{80,96},{96,112},{1,17},{17... | collective-permute-start | bytes 49160 | tf_op jit(solution)/shard_map/ppermute | solution.py:18
  208.6 5.1 collective-permute-start.13
  213.7 5.6 collective-permute-start.14
  218.0 4.5 collective-permute-start.15
  222.7 9.5 %collective-permute-start.16 = (f32[18,18,1]{2,1,0:T(8,128)S(1)}, f32[18,18,1]{2,1,0:T(8,128)S(1)}, u32[]{:S(2)}, u32[]{:S(2)}) collective-permute-start(f32[18,18,1]{2,1,0:T(8,128)S(1)} %get-tuple-element.44), channel_id=1, source_target_pairs={{0,1},{1,2},{2,3},{4,5},{5,6},{6,7},{8,9},{9,10},{10,11},{12,13},{... | collective-permute-start | bytes 3896 | tf_op jit(solution)/shard_map/ppermute | solution.py:18
  227.0 9.1 %collective-permute-start.17 = (f32[18,18,1]{2,1,0:T(8,128)S(1)}, f32[18,18,1]{2,1,0:T(8,128)S(1)}, u32[]{:S(2)}, u32[]{:S(2)}) collective-permute-start(f32[18,18,1]{2,1,0:T(8,128)S(1)} %get-tuple-element.45), channel_id=1, source_target_pairs={{1,0},{2,1},{3,2},{5,4},{6,5},{7,6},{9,8},{10,9},{11,10},{13,12},{... | collective-permute-start | bytes 3896 | tf_op jit(solution)/shard_map/ppermute | solution.py:19
  304.5 76.9 %collective-permute-start.18 = (f32[2,16,256]{2,1,0:T(8,128)S(1)}, f32[2,16,256]{2,1,0:T(8,128)S(1)}, u32[]{:S(2)}, u32[]{:S(2)}) collective-permute-start(f32[2,16,256]{2,1,0:T(8,128)S(1)} %get-tuple-element.56), channel_id=1, source_target_pairs={{0,16},{16,32},{32,48},{48,64},{64,80},{80,96},{96,112},{1,17},{17... | collective-permute-start | bytes 98312 | tf_op jit(solution)/shard_map/ppermute | solution.py:18
  307.5 73.8 %collective-permute-start.19 = (f32[2,16,256]{2,1,0:T(8,128)S(1)}, f32[2,16,256]{2,1,0:T(8,128)S(1)}, u32[]{:S(2)}, u32[]{:S(2)}) collective-permute-start(f32[2,16,256]{2,1,0:T(8,128)S(1)} %get-tuple-element.57), channel_id=1, source_target_pairs={{16,0},{32,16},{48,32},{64,48},{80,64},{96,80},{112,96},{17,1},{33... | collective-permute-start | bytes 98312 | tf_op jit(solution)/shard_map/ppermute | solution.py:19
  381.4 4.2 collective-permute-start.20
  384.1 4.7 collective-permute-start.21
  389.0 9.7 %collective-permute-start.22 = (f32[20,20,2]{2,1,0:T(8,128)S(1)}, f32[20,20,2]{2,1,0:T(8,128)S(1)}, u32[]{:S(2)}, u32[]{:S(2)}) collective-permute-start(f32[20,20,2]{2,1,0:T(8,128)S(1)} %get-tuple-element.38), channel_id=1, source_target_pairs={{0,1},{1,2},{2,3},{4,5},{5,6},{6,7},{8,9},{9,10},{10,11},{12,13},{... | collective-permute-start | bytes 9608 | tf_op jit(solution)/shard_map/ppermute | solution.py:18
  390.8 7.9 %collective-permute-start.23 = (f32[20,20,2]{2,1,0:T(8,128)S(1)}, f32[20,20,2]{2,1,0:T(8,128)S(1)}, u32[]{:S(2)}, u32[]{:S(2)}) collective-permute-start(f32[20,20,2]{2,1,0:T(8,128)S(1)} %get-tuple-element.39), channel_id=1, source_target_pairs={{1,0},{2,1},{3,2},{5,4},{6,5},{7,6},{9,8},{10,9},{11,10},{13,12},{... | collective-permute-start | bytes 9608 | tf_op jit(solution)/shard_map/ppermute | solution.py:19
  405.0 99.2 %copy-start.9 = (f32[3,16,16,256]{3,2,1,0:T(8,128)S(1)}, f32[3,16,16,256]{3,2,1,0:T(8,128)}, u32[]{:S(2)}) copy-start(f32[3,16,16,256]{3,2,1,0:T(8,128)} %param.7) | copy-start | bytes 2359300
  476.9 4.3 collective-permute-start.24
  479.1 5.1 collective-permute-start.25
  484.2 3.8 collective-permute-start.26
  486.6 84.6 %copy-start.11 = (f32[16,16,256]{2,1,0:T(8,128)S(1)}, f32[16,16,256]{2,1,0:T(8,128)}, u32[]{:S(2)}) copy-start(f32[16,16,256]{2,1,0:T(8,128)} %copy-done.10) | copy-start | bytes 786436
  486.6 4.6 collective-permute-start.27
  491.4 7.1 %collective-permute-start.28 = (f32[18,18,1]{2,1,0:T(8,128)S(1)}, f32[18,18,1]{2,1,0:T(8,128)S(1)}, u32[]{:S(2)}, u32[]{:S(2)}) collective-permute-start(f32[18,18,1]{2,1,0:T(8,128)S(1)} %get-tuple-element.42), channel_id=1, source_target_pairs={{0,1},{1,2},{2,3},{4,5},{5,6},{6,7},{8,9},{9,10},{10,11},{12,13},{... | collective-permute-start | bytes 3896 | tf_op jit(solution)/shard_map/ppermute | solution.py:18
  493.3 9.1 %collective-permute-start.29 = (f32[18,18,1]{2,1,0:T(8,128)S(1)}, f32[18,18,1]{2,1,0:T(8,128)S(1)}, u32[]{:S(2)}, u32[]{:S(2)}) collective-permute-start(f32[18,18,1]{2,1,0:T(8,128)S(1)} %get-tuple-element.43), channel_id=1, source_target_pairs={{1,0},{2,1},{3,2},{5,4},{6,5},{7,6},{9,8},{10,9},{11,10},{13,12},{... | collective-permute-start | bytes 3896 | tf_op jit(solution)/shard_map/ppermute | solution.py:19
  (14 other events, 94.5 us)
where the time goes:
time: 581 us; the launch traced here: 572 us
  blocking collectives  323 us (56%)
  starting transfers between devices  73.3 us (13%)
  local copies, waits for them, and re-layouts  55.9 us (10%)
  other arithmetic  55.2 us (10%)
  waiting for transfers between devices  29.9 us (5%)
  matrix products  29.2 us (5%)
    psum x2, blocking collectives, norm_sum(): return lax.psum(value, ('gx', 'gy', 'gz'))  130 us
    unnamed x2, blocking collectives  130 us
    psum x1, blocking collectives, shards(): curvature = lax.psum(local_curve, ('gx', 'gy', 'gz'))  63.2 us
    ppermute x15, starting transfers between devices, padded(): before = lax.ppermute(last, axis, up)  49.5 us
    ppermute x15, starting transfers between devices, padded(): after = lax.ppermute(leading, axis, down)  23.7 us
    ppermute x15, waiting for transfers between devices, padded(): after = lax.ppermute(leading, axis, down)  23.2 us
    concatenate x7, other arithmetic, padded(): value = jnp.concatenate([before, value, after], axis=dim)  21.5 us
    dot_general x2, matrix products, project(): jnp.dot(basis.reshape(basis.shape[0], -1), field.reshape(-1), precision=l...  17.4 us
  transfers between devices with their start and end apart: 30, of which 9 were waited for; matrix products, arithmetic and copies ran while one was open for 13% of the time, Pallas kernels for 0%

commit v1 on v0

--- a/solution.py
+++ b/solution.py
@@ -1,11 +1,22 @@
+import functools
 import jax
 import jax.numpy as jnp
 from jax import lax
 from jax.sharding import PartitionSpec as P
+from jax.lax import psum
 
 SWEEPS = 4
 ITERS = 2
 RELAX = 2.0 / 3.0
+
+
+def attach_copies(local_array, mesh_name, bus_axis):
+    for q in (mesh_name, bus_axis):
+        local_array = psum(local_array, axis_name=q)
+    return local_array
+
+
+mark_lane = functools.partial(attach_copies, mesh_name="gx", bus_axis=("gy", "gz"))
 
 
 def padded(value, sides, width):
@@ -82,7 +93,7 @@
 
 
 def norm_sum(value):
-    return lax.psum(value, ("gx", "gy", "gz"))
+    return mark_lane(value)
 
 
 def shards(right_side, conductance, storage, dirichlet, basis, coarse_inverse):

time: 581 us -> 614 us (1.057)
  blocking collectives: 323 us -> 353 us
    psum x1 -> x2, blocking collectives: 63.2 us -> 132 us  [shards(): curvature = lax.psum(local_curve, ('gx', 'gy', 'gz'))]
    psum x2 -> x4, blocking collectives: 130 us -> 90.6 us  [attach_copies(): local_array = psum(local_array, axis_name=q)]
  transfers between devices with their start and end apart: 30 -> 30, of which waited for: 9 -> 9; matrix products, arithmetic and copies ran while one was open for 13% -> 12% of each run, Pallas kernels for 0% -> 0%
where the time goes in v1:
time: 614 us; the launch traced here: 605 us
  blocking collectives  353 us (57%)
  starting transfers between devices  77.7 us (13%)
  local copies, waits for them, and re-layouts  56.2 us (9%)
  other arithmetic  55.1 us (9%)
  matrix products  29.2 us (5%)
  waiting for transfers between devices  28 us (5%)
    psum x2, blocking collectives, shards(): curvature = lax.psum(local_curve, ('gx', 'gy', 'gz'))  132 us
    unnamed x2, blocking collectives  131 us
    psum x4, blocking collectives, attach_copies(): local_array = psum(local_array, axis_name=q)  90.6 us
    ppermute x15, starting transfers between devices, padded(): before = lax.ppermute(last, axis, up)  52.3 us
    ppermute x15, starting transfers between devices, padded(): after = lax.ppermute(leading, axis, down)  25.3 us
    ppermute x15, waiting for transfers between devices, padded(): after = lax.ppermute(leading, axis, down)  22 us
    concatenate x7, other arithmetic, padded(): value = jnp.concatenate([before, value, after], axis=dim)  21.5 us
    dot_general x2, matrix products, project(): jnp.dot(basis.reshape(basis.shape[0], -1), field.reshape(-1), precision=l...  17.4 us
  transfers between devices with their start and end apart: 30, of which 9 were waited for; matrix products, arithmetic and copies ran while one was open for 12% of the time, Pallas kernels for 0%

profile of v1, /device:TPU:1, one launch (start us, length us, event | category | flops | bytes accessed | tf_op | source)
XLA Modules:
  0.0 605.5 jit_solution(10298334458007961743)
XLA Ops:
  2.9 4.6 collective-permute-start.6
  10.3 3.6 collective-permute-start
  15.8 8.8 %fusion.8 = f32[16]{0:T(128)S(1)} fusion(f32[16,16,16,256]{3,2,1,0:T(8,128)} %param.10, f32[16,16,256,1]{2,1,0,3:T(8,128)} %bitcast.289), kind=kOutput, calls=%fused_computation.14 | convolution fusion | flops 12582912 | bytes 4456512 | tf_op jit(solution)/shard_map/dot_general | solution.py:76
  24.8 66.8 %all-reduce.8 = f32[2048]{0:T(1024)S(1)} all-reduce(f32[2048]{0:T(1024)S(1)} %dynamic-update-slice), channel_id=1, replica_groups=mesh['gx'=8,'gy'=4,'gz'=4] {'gx','gy','gz'}, use_global_device_ids=true, to_apply=%add.8 | all-reduce | flops 2048 | bytes 16384
  92.0 2.4 collective-permute-start.2
  98.7 4.7 collective-permute-start.8
  105.7 5.1 fusion.2
  110.9 8.1 %copy.37 = f32[5,22,16,256]{2,1,3,0:T(8,128)} copy(f32[5,22,16,256]{3,2,1,0:T(8,128)S(1)} %pad_maximum_fusion.2) | data formatting | bytes 3604480 | tf_op jit(solution)/shard_map/concatenate | solution.py:31
  119.0 9.1 %copy.36 = f32[5,22,3,256]{2,1,3,0:T(8,128)} copy(f32[5,22,3,256]{3,1,2,0:T(8,128)} %collective-permute-done.8) | data formatting | bytes 675840 | tf_op jit(solution)/shard_map/ppermute | solution.py:29
  128.2 9.0 %copy.38 = f32[5,22,3,256]{2,1,3,0:T(8,128)} copy(f32[5,22,3,256]{3,1,2,0:T(8,128)} %collective-permute-done.9) | data formatting | bytes 675840 | tf_op jit(solution)/shard_map/ppermute | solution.py:30
  137.2 16.9 %pad_maximum_fusion = f32[5,22,22,256]{2,1,3,0:T(8,128)S(1)} fusion(f32[5,22,3,256]{2,1,3,0:T(8,128)} %copy.38, f32[5,22,16,256]{2,1,3,0:T(8,128)} %copy.37, f32[5,22,3,256]{2,1,3,0:T(8,128)} %copy.36), kind=kLoop, calls=%fused_computation | loop fusion | flops 1239040 | bytes 4956160 | tf_op jit(solution)/shard_map/concatenate | solution.py:31
  154.0 5.4 copy-done.4
  160.2 2.7 collective-permute-start.10
  165.1 4.0 collective-permute-start.4
  170.6 9.2 %copy.40 = f32[5,22,22,256]{3,2,1,0:T(8,128)S(1)} copy(f32[5,22,22,256]{2,1,3,0:T(8,128)} %copy-done.4) | data formatting | bytes 4956160 | tf_op jit(solution)/shard_map/concatenate | solution.py:31
  179.9 3.1 copy.39
  184.9 3.2 pad_maximum_fusion.1
  191.5 3.7 fusion.213
  197.2 2.7 fusion.217
  201.8 2.1 fusion.208
  204.0 4.9 collective-permute-start.12
  208.9 2.3 collective-permute-start.13
  211.2 2.7 collective-permute-done.13
  214.0 4.3 collective-permute-start.14
  219.6 3.2 collective-permute-done.15
  223.0 4.3 collective-permute-start.16
  229.7 2.7 collective-permute-done.16
  232.5 3.9 collective-permute-done.17
  237.1 2.1 multiply_reduce_fusion.2
  239.3 13.0 %psum.42 = f32[]{:T(128)} all-reduce(f32[]{:T(128)} %get-tuple-element.5), channel_id=1, replica_groups=mesh['gx'=8,'gy'=4,'gz'=4] {'gx'}, use_global_device_ids=true, to_apply=%region_1.2 | all-reduce | flops 1 | bytes 8 | tf_op jit(solution)/shard_map/psum | solution.py:15
  252.3 29.7 %psum.43 = f32[]{:T(128)} all-reduce(f32[]{:T(128)} %psum.42), channel_id=1, replica_groups=mesh['gx'=8,'gy'=4,'gz'=4] {'gy','gz'}, use_global_device_ids=true, to_apply=%region_2.3 | all-reduce | flops 1 | bytes 8 | tf_op jit(solution)/shard_map/psum | solution.py:15
  282.0 69.6 %psum.44 = f32[]{:T(128)} all-reduce(f32[]{:T(128)} %get-tuple-element.4), channel_id=1, replica_groups=mesh['gx'=8,'gy'=4,'gz'=4] {'gx','gy','gz'}, use_global_device_ids=true, to_apply=%region_4.5 | all-reduce | flops 1 | bytes 8 | tf_op jit(solution)/shard_map/psum | solution.py:126
  356.2 2.2 collective-permute-start.19
  358.4 8.6 %fusion.11 = f32[16]{0:T(128)S(1)} fusion(f32[16,16,16,256]{3,2,1,0:T(8,128)} %param.10, f32[16,16,256,1]{2,1,0,3:T(8,128)S(1)} %bitcast.285), kind=kOutput, calls=%fused_computation.15 | convolution fusion | flops 12582912 | bytes 4456512 | tf_op jit(solution)/shard_map/dot_general | solution.py:76
  367.3 63.8 %all-reduce.9 = f32[2048]{0:T(1024)S(1)} all-reduce(f32[2048]{0:T(1024)S(1)} %dynamic-update-slice.1), channel_id=1, replica_groups=mesh['gx'=8,'gy'=4,'gz'=4] {'gx','gy','gz'}, use_global_device_ids=true, to_apply=%add.9 | all-reduce | flops 2048 | bytes 16384
  434.6 3.2 collective-permute-done.21
  438.1 2.5 collective-permute-start.22
  442.0 6.4 %fusion = f32[1,16,16,256]{3,0,2,1:T(1,128)S(1)} fusion(f32[16,1,1,1]{0,1,3,2:T(1,128)S(1)} %convolution_bitcast_fusion, f32[16,16,256,16]{2,1,0,3:T(8,128)} %bitcast.283), kind=kOutput, calls=%fused_computation.2 | convolution fusion | flops 12582912 | bytes 4456512 | tf_op jit(solution)/shard_map/dot_general | solution.py:82
  454.8 2.5 multiply_reduce_fusion.1
  457.3 14.9 %psum.45 = f32[]{:T(128)} all-reduce(f32[]{:T(128)} %get-tuple-element.8), channel_id=1, replica_groups=mesh['gx'=8,'gy'=4,'gz'=4] {'gx'}, use_global_device_ids=true, to_apply=%region_6.7 | all-reduce | flops 1 | bytes 8 | tf_op jit(solution)/shard_map/psum | solution.py:15
  472.2 33.0 %psum.46 = f32[]{:T(128)} all-reduce(f32[]{:T(128)} %psum.45), channel_id=1, replica_groups=mesh['gx'=8,'gy'=4,'gz'=4] {'gy','gz'}, use_global_device_ids=true, to_apply=%region_7.8 | all-reduce | flops 1 | bytes 8 | tf_op jit(solution)/shard_map/psum | solution.py:15
  507.5 7.7 %collective-permute-start.24 = (f32[1,16,256]{2,1,0:T(8,128)S(1)}, f32[1,16,256]{2,1,0:T(8,128)S(1)}, u32[]{:S(2)}, u32[]{:S(2)}) collective-permute-start(f32[1,16,256]{2,1,0:T(8,128)S(1)} %get-tuple-element.52), channel_id=1, source_target_pairs={{0,16},{16,32},{32,48},{48,64},{64,80},{80,96},{96,112},{1,17},{17... | collective-permute-start | bytes 49160 | tf_op jit(solution)/shard_map/ppermute | solution.py:29
  515.2 3.1 collective-permute-start.25
  523.0 3.2 collective-permute-done.27
  529.2 3.2 collective-permute-done.28
  532.4 3.8 collective-permute-done.29
  538.0 2.4 multiply_reduce_fusion
  540.4 62.6 %psum.47 = f32[]{:T(128)} all-reduce(f32[]{:T(128)} %get-tuple-element.6), channel_id=1, replica_groups=mesh['gx'=8,'gy'=4,'gz'=4] {'gx','gy','gz'}, use_global_device_ids=true, to_apply=%region_9.10 | all-reduce | flops 1 | bytes 8 | tf_op jit(solution)/shard_map/psum | solution.py:126
  (149 shorter events, 58.3 us)
Async XLA Ops:
  0.6 91.0 %copy-start = (f32[16,2048]{1,0:T(8,128)S(1)}, f32[16,2048]{1,0:T(8,128)}, u32[]{:S(2)}) copy-start(f32[16,2048]{1,0:T(8,128)} %param.11) | copy-start | bytes 393220
  0.6 95.9 %copy-start.15 = (f32[16,16,256]{2,1,0:T(8,128)S(1)}, f32[16,16,256]{2,1,0:T(8,128)}, u32[]{:S(2)}) copy-start(f32[16,16,256]{2,1,0:T(8,128)} %param.8) | copy-start | bytes 786436
  0.7 95.8 %copy-start.7 = (f32[3,16,16,256]{3,2,1,0:T(8,128)S(1)}, f32[3,16,16,256]{3,2,1,0:T(8,128)}, u32[]{:S(2)}) copy-start(f32[3,16,16,256]{3,2,1,0:T(8,128)} %param.7) | copy-start | bytes 2359300
  0.7 91.3 %copy-start.16 = (f32[16,16,256]{2,1,0:T(8,128)S(1)}, f32[16,16,256]{2,1,0:T(8,128)}, u32[]{:S(2)}) copy-start(f32[16,16,256]{2,1,0:T(8,128)} %param.6) | copy-start | bytes 786436
  1.8 96.0 %copy-start.18 = (f32[1,16,16,256]{3,2,1,0:T(8,128)}, f32[1,16,16,256]{3,2,1,0:T(8,128)S(1)}, u32[]{:S(2)}) copy-start(f32[1,16,16,256]{3,2,1,0:T(8,128)S(1)} %fusion.212) | copy-start | bytes 786436
  2.9 92.8 %collective-permute-start.6 = (f32[5,3,16,256]{3,2,1,0:T(8,128)S(1)}, f32[5,3,16,256]{3,2,1,0:T(8,128)S(1)}, u32[]{:S(2)}, u32[]{:S(2)}) collective-permute-start(f32[5,3,16,256]{3,2,1,0:T(8,128)S(1)} %get-tuple-element.34), channel_id=1, source_target_pairs={{0,16},{16,32},{32,48},{48,64},{64,80},{80,96},{96,112},{1,17},{17... | collective-permute-start | bytes 737288 | tf_op jit(solution)/shard_map/ppermute | solution.py:29
  7.6 88.9 %collective-permute-start.7 = (f32[5,3,16,256]{3,2,1,0:T(8,128)S(1)}, f32[5,3,16,256]{3,2,1,0:T(8,128)}, u32[]{:S(2)}, u32[]{:S(2)}) collective-permute-start(f32[5,3,16,256]{3,2,1,0:T(8,128)S(1)} %get-tuple-element.35), channel_id=1, source_target_pairs={{16,0},{32,16},{48,32},{64,48},{80,64},{96,80},{112,96},{17,1},{33... | collective-permute-start | bytes 737288 | tf_op jit(solution)/shard_map/ppermute | solution.py:30
  10.3 81.6 %collective-permute-start = (f32[2,16,256]{2,1,0:T(8,128)S(1)}, f32[2,16,256]{2,1,0:T(8,128)S(1)}, u32[]{:S(2)}, u32[]{:S(2)}) collective-permute-start(f32[2,16,256]{2,1,0:T(8,128)S(1)} %get-tuple-element.59), channel_id=1, source_target_pairs={{0,16},{16,32},{32,48},{48,64},{64,80},{80,96},{96,112},{1,17},{17... | collective-permute-start | bytes 98312 | tf_op jit(solution)/shard_map/ppermute | solution.py:29
  13.9 78.1 %collective-permute-start.1 = (f32[2,16,256]{2,1,0:T(8,128)S(1)}, f32[2,16,256]{2,1,0:T(8,128)S(1)}, u32[]{:S(2)}, u32[]{:S(2)}) collective-permute-start(f32[2,16,256]{2,1,0:T(8,128)S(1)} %get-tuple-element.58), channel_id=1, source_target_pairs={{16,0},{32,16},{48,32},{64,48},{80,64},{96,80},{112,96},{17,1},{33... | collective-permute-start | bytes 98312 | tf_op jit(solution)/shard_map/ppermute | solution.py:30
  92.0 18.8 %copy-start.22 = (f32[20,16,256]{2,1,0:T(8,128)}, f32[20,16,256]{2,1,0:T(8,128)S(1)}, u32[]{:S(2)}) copy-start(f32[20,16,256]{2,1,0:T(8,128)S(1)} %constant_dynamic-update-slice_fusion) | copy-start | bytes 983044
  92.0 18.7 %collective-permute-start.2 = (f32[20,2,256]{2,1,0:T(2,128)S(1)}, f32[20,2,256]{2,1,0:T(2,128)S(1)}, u32[]{:S(2)}, u32[]{:S(2)}) collective-permute-start(f32[20,2,256]{2,1,0:T(2,128)S(1)} %get-tuple-element.46), channel_id=1, source_target_pairs={{0,4},{4,8},{8,12},{1,5},{5,9},{9,13},{2,6},{6,10},{10,14},{3,7},{... | collective-permute-start | bytes 122888 | tf_op jit(solution)/shard_map/ppermute | solution.py:29
  94.5 16.3 %collective-permute-start.3 = (f32[20,2,256]{2,1,0:T(2,128)S(1)}, f32[20,2,256]{2,1,0:T(2,128)S(1)}, u32[]{:S(2)}, u32[]{:S(2)}) collective-permute-start(f32[20,2,256]{2,1,0:T(2,128)S(1)} %get-tuple-element.47), channel_id=1, source_target_pairs={{4,0},{8,4},{12,8},{5,1},{9,5},{13,9},{6,2},{10,6},{14,10},{7,3},{... | collective-permute-start | bytes 122888 | tf_op jit(solution)/shard_map/ppermute | solution.py:30
  98.7 20.3 %collective-permute-start.8 = (f32[5,22,3,256]{3,1,2,0:T(8,128)}, f32[5,22,3,256]{3,1,2,0:T(8,128)}, u32[]{:S(2)}, u32[]{:S(2)}) collective-permute-start(f32[5,22,3,256]{3,1,2,0:T(8,128)} %copy.55), channel_id=1, source_target_pairs={{0,4},{4,8},{8,12},{1,5},{5,9},{9,13},{2,6},{6,10},{10,14},{3,7},{... | collective-permute-start | bytes 1013768 | tf_op jit(solution)/shard_map/ppermute | solution.py:29
  104.2 23.9 %collective-permute-start.9 = (f32[5,22,3,256]{3,1,2,0:T(8,128)}, f32[5,22,3,256]{3,1,2,0:T(8,128)}, u32[]{:S(2)}, u32[]{:S(2)}) collective-permute-start(f32[5,22,3,256]{3,1,2,0:T(8,128)} %copy.56), channel_id=1, source_target_pairs={{4,0},{8,4},{12,8},{5,1},{9,5},{13,9},{6,2},{10,6},{14,10},{7,3},{... | collective-permute-start | bytes 1013768 | tf_op jit(solution)/shard_map/ppermute | solution.py:30
  160.2 19.6 %collective-permute-start.10 = (f32[5,22,22,3]{2,1,3,0:T(8,128)}, f32[5,22,22,3]{2,1,3,0:T(8,128)}, u32[]{:S(2)}, u32[]{:S(2)}) collective-permute-start(f32[5,22,22,3]{2,1,3,0:T(8,128)} %get-tuple-element.28), channel_id=1, source_target_pairs={{0,1},{1,2},{2,3},{4,5},{5,6},{6,7},{8,9},{9,10},{10,11},{12,13},{... | collective-permute-start | bytes 87128 | tf_op jit(solution)/shard_map/ppermute | solution.py:29
  162.9 20.0 %collective-permute-start.11 = (f32[5,22,22,3]{2,1,3,0:T(8,128)}, f32[5,22,22,3]{2,1,3,0:T(8,128)S(1)}, u32[]{:S(2)}, u32[]{:S(2)}) collective-permute-start(f32[5,22,22,3]{2,1,3,0:T(8,128)} %get-tuple-element.29), channel_id=1, source_target_pairs={{1,0},{2,1},{3,2},{5,4},{6,5},{7,6},{9,8},{10,9},{11,10},{13,12},{... | collective-permute-start | bytes 87128 | tf_op jit(solution)/shard_map/ppermute | solution.py:30
  165.1 25.7 %collective-permute-start.4 = (f32[20,20,2]{2,1,0:T(8,128)}, f32[20,20,2]{2,1,0:T(8,128)S(1)}, u32[]{:S(2)}, u32[]{:S(2)}) collective-permute-start(f32[20,20,2]{2,1,0:T(8,128)} %get-tuple-element.38), channel_id=1, source_target_pairs={{0,1},{1,2},{2,3},{4,5},{5,6},{6,7},{8,9},{9,10},{10,11},{12,13},{... | collective-permute-start | bytes 9608 | tf_op jit(solution)/shard_map/ppermute | solution.py:29
  169.1 22.4 %collective-permute-start.5 = (f32[20,20,2]{2,1,0:T(8,128)}, f32[20,20,2]{2,1,0:T(8,128)}, u32[]{:S(2)}, u32[]{:S(2)}) collective-permute-start(f32[20,20,2]{2,1,0:T(8,128)} %get-tuple-element.39), channel_id=1, source_target_pairs={{1,0},{2,1},{3,2},{5,4},{6,5},{7,6},{9,8},{10,9},{11,10},{13,12},{... | collective-permute-start | bytes 9608 | tf_op jit(solution)/shard_map/ppermute | solution.py:30
  188.1 48.3 %copy-start.1 = (f32[5,22,22,262]{3,2,1,0:T(8,128)}, f32[5,22,22,262]{3,2,1,0:T(8,128)S(1)}, u32[]{:S(2)}) copy-start(f32[5,22,22,262]{3,2,1,0:T(8,128)S(1)} %pad_maximum_fusion.1) | copy-start | bytes 7608484
  201.7 37.6 %copy-start.21 = (f32[20,20,260]{2,1,0:T(8,128)}, f32[20,20,260]{2,1,0:T(8,128)S(1)}, u32[]{:S(2)}) copy-start(f32[20,20,260]{2,1,0:T(8,128)S(1)} %get-tuple-element.30) | copy-start | bytes 1248004
  201.7 35.3 %copy-start.6 = (f32[5,22,22,256]{3,2,1,0:T(8,128)S(1)}, f32[5,22,22,256]{3,2,1,0:T(8,128)}, u32[]{:S(2)}) copy-start(f32[5,22,22,256]{3,2,1,0:T(8,128)} %copy-done.5) | copy-start | bytes 7434244
  201.7 35.3 %copy-start.8 = (f32[3,16,16,256]{3,2,1,0:T(8,128)S(1)}, f32[3,16,16,256]{3,2,1,0:T(8,128)}, u32[]{:S(2)}) copy-start(f32[3,16,16,256]{3,2,1,0:T(8,128)} %param.7) | copy-start | bytes 2359300
  201.7 35.3 %copy-start.12 = (f32[5,22,22,3]{3,2,1,0:T(8,128)S(1)}, f32[5,22,22,3]{3,2,1,0:T(8,128)}, u32[]{:S(2)}) copy-start(f32[5,22,22,3]{3,2,1,0:T(8,128)} %copy.39) | copy-start | bytes 87124
  201.7 35.3 %copy-start.17 = (f32[16,16,256]{2,1,0:T(8,128)S(1)}, f32[16,16,256]{2,1,0:T(8,128)}, u32[]{:S(2)}) copy-start(f32[16,16,256]{2,1,0:T(8,128)} %param.6) | copy-start | bytes 786436
  201.8 35.3 %copy-start.19 = (f32[1,16,16,256]{3,2,1,0:T(8,128)S(1)}, f32[1,16,16,256]{3,2,1,0:T(8,128)}, u32[]{:S(2)}) copy-start(f32[1,16,16,256]{3,2,1,0:T(8,128)} %copy-done.18) | copy-start | bytes 786436
  201.8 35.3 %copy-start.20 = (s32[16,16,256]{2,1,0:T(8,128)S(1)}, s32[16,16,256]{2,1,0:T(8,128)}, u32[]{:S(2)}) copy-start(s32[16,16,256]{2,1,0:T(8,128)} %param.9) | copy-start | bytes 786436
  201.8 35.3 %copy-start.26 = (f32[5,3,16,256]{3,2,1,0:T(8,128)S(1)}, f32[5,3,16,256]{3,2,1,0:T(8,128)}, u32[]{:S(2)}) copy-start(f32[5,3,16,256]{3,2,1,0:T(8,128)} %copy-done.25) | copy-start | bytes 737284
  203.9 35.3 %copy-start.10 = (f32[16,16,256]{2,1,0:T(8,128)}, f32[16,16,256]{2,1,0:T(8,128)S(1)}, u32[]{:S(2)}) copy-start(f32[16,16,256]{2,1,0:T(8,128)S(1)} %fusion.208) | copy-start | bytes 786436
  204.0 7.3 %collective-permute-start.12 = (f32[1,16,256]{2,1,0:T(8,128)S(1)}, f32[1,16,256]{2,1,0:T(8,128)S(1)}, u32[]{:S(2)}, u32[]{:S(2)}) collective-permute-start(f32[1,16,256]{2,1,0:T(8,128)S(1)} %get-tuple-element.56), channel_id=1, source_target_pairs={{0,16},{16,32},{32,48},{48,64},{64,80},{80,96},{96,112},{1,17},{17... | collective-permute-start | bytes 49160 | tf_op jit(solution)/shard_map/ppermute | solution.py:29
  208.9 5.1 collective-permute-start.13
  214.0 5.6 collective-permute-start.14
  218.3 4.5 collective-permute-start.15
  223.0 9.5 %collective-permute-start.16 = (f32[18,18,1]{2,1,0:T(8,128)S(1)}, f32[18,18,1]{2,1,0:T(8,128)S(1)}, u32[]{:S(2)}, u32[]{:S(2)}) collective-permute-start(f32[18,18,1]{2,1,0:T(8,128)S(1)} %get-tuple-element.42), channel_id=1, source_target_pairs={{0,1},{1,2},{2,3},{4,5},{5,6},{6,7},{8,9},{9,10},{10,11},{12,13},{... | collective-permute-start | bytes 3896 | tf_op jit(solution)/shard_map/ppermute | solution.py:29
  227.2 9.1 %collective-permute-start.17 = (f32[18,18,1]{2,1,0:T(8,128)S(1)}, f32[18,18,1]{2,1,0:T(8,128)S(1)}, u32[]{:S(2)}, u32[]{:S(2)}) collective-permute-start(f32[18,18,1]{2,1,0:T(8,128)S(1)} %get-tuple-element.43), channel_id=1, source_target_pairs={{1,0},{2,1},{3,2},{5,4},{6,5},{7,6},{9,8},{10,9},{11,10},{13,12},{... | collective-permute-start | bytes 3896 | tf_op jit(solution)/shard_map/ppermute | solution.py:30
  354.1 77.0 %collective-permute-start.18 = (f32[2,16,256]{2,1,0:T(8,128)S(1)}, f32[2,16,256]{2,1,0:T(8,128)S(1)}, u32[]{:S(2)}, u32[]{:S(2)}) collective-permute-start(f32[2,16,256]{2,1,0:T(8,128)S(1)} %get-tuple-element.54), channel_id=1, source_target_pairs={{0,16},{16,32},{32,48},{48,64},{64,80},{80,96},{96,112},{1,17},{17... | collective-permute-start | bytes 98312 | tf_op jit(solution)/shard_map/ppermute | solution.py:29
  356.2 74.9 %collective-permute-start.19 = (f32[2,16,256]{2,1,0:T(8,128)S(1)}, f32[2,16,256]{2,1,0:T(8,128)S(1)}, u32[]{:S(2)}, u32[]{:S(2)}) collective-permute-start(f32[2,16,256]{2,1,0:T(8,128)S(1)} %get-tuple-element.55), channel_id=1, source_target_pairs={{16,0},{32,16},{48,32},{64,48},{80,64},{96,80},{112,96},{17,1},{33... | collective-permute-start | bytes 98312 | tf_op jit(solution)/shard_map/ppermute | solution.py:30
  431.1 3.5 collective-permute-start.20
  433.1 4.7 collective-permute-start.21
  438.1 10.4 %collective-permute-start.22 = (f32[20,20,2]{2,1,0:T(8,128)S(1)}, f32[20,20,2]{2,1,0:T(8,128)S(1)}, u32[]{:S(2)}, u32[]{:S(2)}) collective-permute-start(f32[20,20,2]{2,1,0:T(8,128)S(1)} %get-tuple-element.36), channel_id=1, source_target_pairs={{0,1},{1,2},{2,3},{4,5},{5,6},{6,7},{8,9},{9,10},{10,11},{12,13},{... | collective-permute-start | bytes 9608 | tf_op jit(solution)/shard_map/ppermute | solution.py:29
  440.5 7.9 %collective-permute-start.23 = (f32[20,20,2]{2,1,0:T(8,128)S(1)}, f32[20,20,2]{2,1,0:T(8,128)S(1)}, u32[]{:S(2)}, u32[]{:S(2)}) collective-permute-start(f32[20,20,2]{2,1,0:T(8,128)S(1)} %get-tuple-element.37), channel_id=1, source_target_pairs={{1,0},{2,1},{3,2},{5,4},{6,5},{7,6},{9,8},{10,9},{11,10},{13,12},{... | collective-permute-start | bytes 9608 | tf_op jit(solution)/shard_map/ppermute | solution.py:30
  454.8 83.2 %copy-start.9 = (f32[3,16,16,256]{3,2,1,0:T(8,128)S(1)}, f32[3,16,16,256]{3,2,1,0:T(8,128)}, u32[]{:S(2)}) copy-start(f32[3,16,16,256]{3,2,1,0:T(8,128)} %param.7) | copy-start | bytes 2359300
  507.5 10.8 %collective-permute-start.24 = (f32[1,16,256]{2,1,0:T(8,128)S(1)}, f32[1,16,256]{2,1,0:T(8,128)S(1)}, u32[]{:S(2)}, u32[]{:S(2)}) collective-permute-start(f32[1,16,256]{2,1,0:T(8,128)S(1)} %get-tuple-element.52), channel_id=1, source_target_pairs={{0,16},{16,32},{32,48},{48,64},{64,80},{80,96},{96,112},{1,17},{17... | collective-permute-start | bytes 49160 | tf_op jit(solution)/shard_map/ppermute | solution.py:29
  515.2 5.1 collective-permute-start.25
  520.3 2.7 collective-permute-start.26
  521.6 82.8 %copy-start.11 = (f32[16,16,256]{2,1,0:T(8,128)S(1)}, f32[16,16,256]{2,1,0:T(8,128)}, u32[]{:S(2)}) copy-start(f32[16,16,256]{2,1,0:T(8,128)} %copy-done.10) | copy-start | bytes 786436
  521.6 4.6 collective-permute-start.27
  526.4 6.0 collective-permute-start.28
  527.7 8.5 %collective-permute-start.29 = (f32[18,18,1]{2,1,0:T(8,128)S(1)}, f32[18,18,1]{2,1,0:T(8,128)S(1)}, u32[]{:S(2)}, u32[]{:S(2)}) collective-permute-start(f32[18,18,1]{2,1,0:T(8,128)S(1)} %get-tuple-element.41), channel_id=1, source_target_pairs={{1,0},{2,1},{3,2},{5,4},{6,5},{7,6},{9,8},{10,9},{11,10},{13,12},{... | collective-permute-start | bytes 3896 | tf_op jit(solution)/shard_map/ppermute | solution.py:30
  (14 other events, 94.6 us)
